TPU v7x, 32 devices: a whole 2x2x4 slice. The times are simulated.
32 devices in a mesh: sym: 4 (over x, core), row: 8 (over z, y).
Axes of the slice: x: 2, y: 2, z: 4, core: 2. Of those that a mesh axis runs over, the one named last changes fastest.
Arguments:
- vectors: float32 [4, 32768, 256], P('sym', 'row'), may hold values from -6 to 6
- reflectors: float32 [4, 32768, 512], P('sym', 'row'), may hold values from -0.5 to 0.5
- factors: float32 [4, 4, 128, 128], P('sym'), may hold values from -0.03125 to 0.03125
- tiles: bfloat16 [4, 16, 512, 512], P('sym', 'row'), may hold values from -0.0029296875 to 0.0029296875
- tile_left: int32 [4, 16], P('sym', 'row'), may hold values from 0 to 7
- tile_right: int32 [4, 16], P('sym', 'row'), may hold values from 0 to 7
- tile_occupied_mask: int32 [4, 16], P('sym', 'row'), may hold values 0 or 1
- channels: int32 [4, 64], P('sym', 'row'), may hold values from 256 to 512
Outputs:
- dipole: float32 [4, 256, 256], P('sym', 'row')
All inputs are finite; a program needn't handle non-finite values. No bound on the sum of `tile_occupied_mask` on one device may be relied on, other than what follows from the above.
Results may differ from a plain program's by a relative error of at most 0.0049.
Values may be sent and summed in bfloat16 or wider, within the bound.
A program may use at most 64 MiB of HBM per device.

v0:
```python
import jax
import jax.numpy as jnp
from jax import lax
from jax.sharding import PartitionSpec as P

BLOCK = 512


PRECISE = lax.Precision.HIGHEST


def passed_along(block, axis, distance):
    devices = range(lax.axis_size(axis))
    route = [((i - distance) % len(devices), i) for i in devices]
    return lax.ppermute(block, axis, route)


def row_inner(first, second):
    return lax.dot_general(first, second, (((0,), (0,)), ((), ())), precision=PRECISE)


def on_device(
    vectors, reflectors, factors, tiles, tile_left, tile_right, tile_occupied_mask, channels
):
    start = vectors[0]
    panels = reflectors[0]
    factor_set = factors[0]
    panel_count = factor_set.shape[0]
    panel_width = factor_set.shape[1]
    pieces = []
    for level in range(panel_count - 1):
        panel = panels[:, level * panel_width : (level + 1) * panel_width]
        pieces.append(row_inner(panel, panels[:, (level + 1) * panel_width :]).reshape(-1))
    coupled, projected = lax.psum(
        (jnp.concatenate(pieces, axis=0), row_inner(panels, start)), "row"
    )
    uppers = []
    offset = 0
    for level in range(panel_count - 1):
        later_width = (panel_count - 1 - level) * panel_width
        uppers.append(
            coupled[offset : offset + panel_width * later_width].reshape(panel_width, later_width)
        )
        offset = offset + panel_width * later_width
    updates = [None] * panel_count
    for level in reversed(range(panel_count)):
        current = projected[level * panel_width : (level + 1) * panel_width]
        for later in range(level + 1, panel_count):
            begin = (later - level - 1) * panel_width
            coupling = uppers[level][:, begin : begin + panel_width]
            current = current - jnp.dot(coupling, updates[later], precision=PRECISE)
        updates[level] = jnp.dot(factor_set[level], current, precision=PRECISE)
    result = start - jnp.dot(panels, jnp.concatenate(updates, axis=0), precision=PRECISE)
    eigen_count = result.shape[1]
    position = jnp.arange(BLOCK, dtype=jnp.int32)
    keeper = (position[None, :] < channels[0][:, None]).astype(jnp.float32)
    masked = (result.reshape(-1, BLOCK, eigen_count) * keeper[:, :, None]).astype(jnp.bfloat16)
    slots = tile_right[0]
    remote = passed_along(masked, "sym", -1)
    right_rows = jnp.take(remote, slots, axis=0)
    bra_state_rows = (
        jnp.take(masked, tile_left[0], axis=0)
        * tile_occupied_mask[0].astype(jnp.bfloat16)[:, None, None]
    )
    bra_ket_product = jnp.einsum(
        "tij,tjk->tik", tiles[0], right_rows, preferred_element_type=jnp.float32
    ).astype(jnp.bfloat16)
    partial_sum = jnp.einsum(
        "tji,tjk->ik", bra_state_rows, bra_ket_product, preferred_element_type=jnp.float32
    )
    total = lax.psum(partial_sum, "row")
    share_rows = eigen_count // lax.axis_size("row")
    shares = lax.dynamic_slice_in_dim(total, lax.axis_index("row") * share_rows, share_rows, 0)
    return shares[None]


def solution(mesh):
    return jax.shard_map(
        on_device,
        mesh=mesh,
        in_specs=(
            P("sym", "row", None),
            P("sym", "row", None),
            P("sym", None, None, None),
            P("sym", "row", None, None),
            P("sym", "row"),
            P("sym", "row"),
            P("sym", "row"),
            P("sym", "row"),
        ),
        out_specs=P("sym", "row", None),
        check_vma=False,
    )
```

profile of v0, /device:TPU:1, one launch (start us, length us, event | category | flops | bytes accessed | tf_op | source)
XLA Modules:
  0.0 259.1 jit_solution(3938977497541981801)
XLA Ops:
  6.5 8.1 %fusion = f32[128,384]{1,0:T(8,128)S(1)} fusion(f32[4096,512]{1,0:T(8,128)} %bitcast.74), kind=kOutput, calls=%fused_computation.2 | convolution fusion | flops 2415919104 | bytes 8585216 | tf_op jit(solution)/shard_map/dot_general | solution.py:19
  14.7 3.5 %fusion.14 = f32[16,2,8,128]{3,2,1,0:T(8,128)S(1)} fusion(f32[4096,512]{1,0:T(8,128)S(1)} %bitcast.75), kind=kOutput, calls=%fused_computation.20 | convolution fusion | flops 1610612736 | bytes 6422528 | tf_op jit(solution)/shard_map/dot_general | solution.py:19
  18.2 3.4 %convolution_bitcast_fusion.1 = f32[16384]{0:T(1024)S(1)} fusion(f32[4096,512]{1,0:T(8,128)S(1)} %bitcast.76), kind=kOutput, calls=%fused_computation.11 | convolution fusion | flops 805306368 | bytes 4259840 | tf_op jit(solution)/shard_map/dot_general | solution.py:19
  21.7 0.1 copy.15
  21.8 17.2 %fusion.5 = f32[512,256]{1,0:T(8,128)} fusion(f32[1,4096,256]{2,1,0:T(8,128)} %param.10, f32[1,4096,512]{2,1,0:T(8,128)} %param.11), kind=kOutput, calls=%fused_computation.8 | convolution fusion | flops 6442450944 | bytes 13107200 | tf_op jit(solution)/shard_map/dot_general | solution.py:19
  38.9 0.8 pad_maximum_fusion
  39.8 0.0 all-reduce.4.cloned.1.call-start
  39.8 5.7 %copy.10 = f32[1,4096,256]{1,2,0:T(8,128)} copy(f32[1,4096,256]{2,1,0:T(8,128)} %param.10) | data formatting | bytes 8388608 | tf_op args[0]
  45.5 0.1 fusion.53
  45.6 71.9 %all-reduce.6.cloned.1.call-done = (f32[512,256]{1,0:T(8,128)}, f32[98304]{0:T(1024)}) async-done(((f32[512,256]{1,0:T(8,128)}, f32[98304]{0:T(1024)}), (f32[512,256]{1,0:T(8,128)}, f32[98304]{0:T(1024)})) %all-reduce.6.cloned.1.call-update) | async-done | bytes 917520 | tf_op jit(solution)/shard_map/psum | solution.py:34
  117.5 0.9 slice.139
  118.4 0.9 slice.136
  119.4 1.2 fusion.36
  120.6 1.2 convolution_subtract_fusion.5
  121.8 0.3 fusion.46
  122.1 1.2 convolution_subtract_fusion.4
  123.3 0.3 convolution_subtract_fusion.3
  123.5 0.3 fusion.44
  123.9 1.2 convolution_subtract_fusion.2
  125.0 0.3 convolution_subtract_fusion.1
  125.3 0.3 convolution_subtract_fusion
  125.6 0.3 convolution_bitcast_fusion.2
  125.9 18.1 %fusion.2 = f32[4096,256]{0,1:T(8,128)} fusion(f32[1,4096,256]{1,2,0:T(8,128)} %copy.10, f32[128,256]{1,0:T(8,128)S(1)} %bitcast.78, f32[128,256]{1,0:T(8,128)S(1)} %bitcast.79, f32[128,256]{1,0:T(8,128)S(1)} %bitcast.80, f32[128,256]{1,0:T(8,128)S(1)} %convolution_bitcast_fusion.2, f32[1,4096,512]{2,1,0:T(8,128)} %param.11), kind=kOutput, calls=%fused_computation.5 | convolution fusion | flops 6443892736 | bytes 17301504 | tf_op jit(solution)/shard_map/dot_general | solution.py:53
  144.0 5.6 %copy.14 = f32[4096,256]{1,0:T(8,128)} copy(f32[4096,256]{0,1:T(8,128)} %fusion.2) | data formatting | bytes 8388608 | tf_op jit(solution)/shard_map/reshape | solution.py:57
  149.6 2.6 %multiply_convert_fusion = bf16[8,512,256]{2,1,0:T(8,128)(2,1)S(1)} fusion(f32[8,512,256]{2,1,0:T(8,128)} %bitcast.77, f32[8,512]{1,0:T(8,128)S(1)} %fusion.53), kind=kLoop, calls=%fused_computation.10 | loop fusion | flops 2097152 | bytes 6307840 | tf_op jit(solution)/shard_map/convert_element_type | solution.py:57
  152.2 1.7 collective-permute-start
  154.1 1.4 gather_fusion
  155.4 23.7 %collective-permute-done = bf16[8,512,256]{2,1,0:T(8,128)(2,1)} collective-permute-done((bf16[8,512,256]{2,1,0:T(8,128)(2,1)S(1)}, bf16[8,512,256]{2,1,0:T(8,128)(2,1)}, u32[]{:S(2)}, u32[]{:S(2)}) %collective-permute-start) | collective-permute-done | bytes 2097184 | tf_op jit(solution)/shard_map/ppermute | solution.py:15
  179.1 2.2 gather_fusion.1
  181.3 2.6 fusion.13
  183.9 67.0 %all-reduce.4.cloned.1.call-done = f32[256,256]{1,0:T(8,128)} async-done(((f32[256,256]{1,0:T(8,128)}), f32[256,256]{1,0:T(8,128)}) %all-reduce.4.cloned.1.call-update) | async-done | bytes 262160 | tf_op jit(solution)/shard_map/psum | solution.py:71
  250.9 1.4 dynamic-slice_bitcast_fusion
  (26 shorter events, 0.2 us)
Async XLA Ops:
  6.5 174.7 %copy-start = (bf16[1,2,512,512]{3,2,1,0:T(8,128)(2,1)S(1)}, bf16[1,2,512,512]{3,2,1,0:T(8,128)(2,1)}, u32[]{:S(2)}) copy-start(bf16[1,2,512,512]{3,2,1,0:T(8,128)(2,1)} %param.13) | copy-start | bytes 3145732
  6.5 111.0 %all-reduce.6.cloned.1.call-start = ((), (), s32[]{:S(2)}) async-start(), calls=%async_computation.1 | async-start | bytes 1835008 | tf_op jit(solution)/shard_map/psum | solution.py:34
  6.5 8.1 %copy-start.1 = (f32[1,4096,512]{2,1,0:T(8,128)S(1)}, f32[1,4096,512]{2,1,0:T(8,128)}, u32[]{:S(2)}) copy-start(f32[1,4096,512]{2,1,0:T(8,128)} %param.11) | copy-start | bytes 25165828
  39.7 5.8 %copy-start.3 = (s32[1,8]{1,0:T(1,128)S(1)}, s32[1,8]{1,0:T(1,128)}, u32[]{:S(2)}) copy-start(s32[1,8]{1,0:T(1,128)} %param.17) | copy-start | bytes 100
  39.8 79.6 %copy-start.2 = (f32[1,4,128,128]{3,2,1,0:T(8,128)S(1)}, f32[1,4,128,128]{3,2,1,0:T(8,128)}, u32[]{:S(2)}) copy-start(f32[1,4,128,128]{3,2,1,0:T(8,128)} %param.12) | copy-start | bytes 786436
  39.8 211.2 %all-reduce.4.cloned.1.call-start = ((), (), s32[]{:S(2)}) async-start(), calls=%async_computation | async-start | bytes 524288 | tf_op jit(solution)/shard_map/psum | solution.py:71
  149.6 4.4 %copy-start.4 = (s32[1,2]{1,0:T(1,128)S(1)}, s32[1,2]{1,0:T(1,128)}, u32[]{:S(2)}) copy-start(s32[1,2]{1,0:T(1,128)} %param.15) | copy-start | bytes 28
  149.6 4.4 %copy-start.5 = (s32[1,2]{1,0:T(1,128)S(1)}, s32[1,2]{1,0:T(1,128)}, u32[]{:S(2)}) copy-start(s32[1,2]{1,0:T(1,128)} %param.14) | copy-start | bytes 28
  149.6 4.4 %copy-start.6 = (s32[1,2]{1,0:T(1,128)S(1)}, s32[1,2]{1,0:T(1,128)}, u32[]{:S(2)}) copy-start(s32[1,2]{1,0:T(1,128)} %param.16) | copy-start | bytes 28
  152.2 26.8 %collective-permute-start = (bf16[8,512,256]{2,1,0:T(8,128)(2,1)S(1)}, bf16[8,512,256]{2,1,0:T(8,128)(2,1)}, u32[]{:S(2)}, u32[]{:S(2)}) collective-permute-start(bf16[8,512,256]{2,1,0:T(8,128)(2,1)S(1)} %multiply_convert_fusion), channel_id=1, source_target_pairs={{8,0},{16,8},{24,16},{0,24},{9,1},{17,9},{25,17},{1,25},{10,2},{18... | collective-permute-start | bytes 6291464 | tf_op jit(solution)/shard_map/ppermute | solution.py:15
Sparse Core Ops, SparseCore 0:
  39.9 77.5 all-reduce.5
  184.0 66.8 all-reduce.3
where the time goes:
time: 262 us; the launch traced here: 259 us
  waiting for transfers between devices  163 us (62%)
  matrix products  59.3 us (23%)
  local copies, waits for them, and re-layouts  18.3 us (7%)
  between operations  13.6 us (5%)
  other arithmetic  3.51 us (1%)
    psum x1, waiting for transfers between devices, on_device(): lax.psum((jnp.concatenate(pieces, axis=0), row_inner(panels, start)), 'row')  71.9 us
    psum x1, waiting for transfers between devices, on_device(): total = lax.psum(partial_sum, 'row')  67 us
    dot_general x4, matrix products, row_inner(): lax.dot_general(first, second, (((0,), (0,)), ((), ())), precision=PRECISE)  32.3 us
    ppermute x1, waiting for transfers between devices, passed_along(): return lax.ppermute(block, axis, route)  23.7 us
    dot_general x1, matrix products, on_device(): jnp.dot(panels, jnp.concatenate(updates, axis=0), precision=PRECISE)  18.1 us
    unnamed x16, local copies, waits for them, and re-layouts  5.78 us
    reshape x1, local copies, waits for them, and re-layouts, on_device(): result.reshape(-1, BLOCK, eigen_count) * keeper[:, :, None]  5.63 us
  transfers between devices with their start and end apart: 3, of which 3 were waited for; matrix products, arithmetic and copies ran while one was open for 3% of the time, Pallas kernels for 0%

commit v1 on v0

v1 whole, which is shorter than its diff:
```python
import functools

import jax
import jax.numpy as jnp
from jax import lax
from jax.experimental import pallas as pl
from jax.experimental.pallas import tpu as pltpu
from jax.sharding import PartitionSpec as P

BLOCK = 512
F32 = jnp.float32
BF16 = jnp.bfloat16
MESH = pl.DeviceIdType.MESH


def split(value):
    high = value.astype(BF16)
    return high, (value - high.astype(F32)).astype(BF16)


def contract(first, second, dims):
    high, low = first
    other_high, other_low = second

    def dot(a, b):
        return lax.dot_general(a, b, (dims, ((), ())), preferred_element_type=F32)

    return dot(high, other_high) + (dot(high, other_low) + dot(low, other_high))


ROWS = ((0,), (0,))
PLAIN = ((1,), (0,))
COLUMNS = ((1,), (1,))


def coupled_ranges(first, count):
    if count < 2:
        return []
    half = count // 2
    here = [(first, half, first + half, count - half)]
    return here + coupled_ranges(first, half) + coupled_ranges(first + half, count - half)


def kernel(
    n,
    syms,
    x_hbm,
    v_hbm,
    f_ref,
    tiles_ref,
    right_ref,
    left_ref,
    occupied_ref,
    channels_ref,
    out_ref,
    x_buf,
    v_buf,
    v_high,
    v_low,
    slots_vmem,
    slots_smem,
    partial,
    landed,
    full,
    t_ref,
    u_high,
    u_low,
    ket_out,
    ket_in,
    own,
    dipole_out,
    dipole_in,
    x_sem,
    v_sem,
    slot_sem,
    reduce_send,
    reduce_recv,
    ket_send,
    ket_recv,
    dipole_send,
    dipole_recv,
):
    panels, width, _ = f_ref.shape
    blocks, _, eig = x_buf.shape
    tile_slots = tiles_ref.shape[0]
    steps = n.bit_length() - 1
    sym = lax.axis_index("sym")
    me = lax.axis_index("row")
    after = lax.rem(sym + 1, syms)
    before = lax.rem(sym + syms - 1, syms)

    def load(source, target, sems, r):
        return pltpu.make_async_copy(source.at[r], target.at[r], sems.at[r])

    for r in range(blocks):
        load(v_hbm, v_buf, v_sem, r).start()
    for r in range(blocks):
        load(x_hbm, x_buf, x_sem, r).start()

    barrier = pltpu.get_barrier_semaphore()
    for d in range(1, n):
        pl.semaphore_signal(
            barrier, inc=1, device_id=(sym, lax.rem(me + d, n)), device_id_type=MESH
        )
    for other in (after, before):
        pl.semaphore_signal(barrier, inc=1, device_id=(other, me), device_id_type=MESH)
    pl.semaphore_wait(barrier, n + 1)

    slots_copy = pltpu.make_async_remote_copy(
        src_ref=right_ref,
        dst_ref=slots_vmem,
        send_sem=slot_sem.at[0],
        recv_sem=slot_sem.at[1],
        device_id=(after, me),
        device_id_type=MESH,
    )
    slots_copy.start()

    ranges = coupled_ranges(0, panels)

    def couple(r, sums):
        load(v_hbm, v_buf, v_sem, r).wait()
        high, low = split(v_buf[r])
        v_high[r] = high
        v_low[r] = low
        out = []
        for total, (a, ca, b, cb) in zip(sums, ranges):
            pa = slice(a * width, (a + ca) * width)
            pb = slice(b * width, (b + cb) * width)
            out.append(
                total + contract((high[:, pa], low[:, pa]), (high[:, pb], low[:, pb]), ROWS)
            )
        return tuple(out)

    sums = lax.fori_loop(
        0, blocks, couple, tuple(jnp.zeros((ca * width, cb * width), F32) for _, ca, _, cb in ranges)
    )
    where = {}
    place = 0
    firsts = []
    for total, (a, ca, b, cb) in zip(sums, ranges):
        for i in range(ca):
            for j in range(cb):
                where[(a + i, b + j)] = place
                partial[place : place + width, :] = total[
                    i * width : (i + 1) * width, j * width : (j + 1) * width
                ]
                place = place + width
        firsts.append(place)
    coupled_rows = place
    jobs = [(0, firsts[0]), (firsts[0], coupled_rows - firsts[0])]
    group = panels // 2
    for begin in range(0, panels, group):
        jobs.append((coupled_rows + begin * eig, group * eig))

    copies = {}

    def offset_after(job, count):
        base, size = jobs[job]
        offset = base
        for b in range(count):
            offset = offset + lax.rem(me // (1 << b), 2) * (size >> (b + 1))
        return offset

    def aligned(offset, length):
        return pl.ds(pl.multiple_of(offset, 8), length)

    def start(job, phase):
        base, size = jobs[job]
        b = phase if phase < steps else 2 * steps - 1 - phase
        bit = lax.rem(me // (1 << b), 2)
        partner = me + (1 - 2 * bit) * (1 << b)
        half = size >> (b + 1)
        if phase < steps:
            source = partial.at[aligned(offset_after(job, b) + (1 - bit) * half, half)]
            slot = base + size - 2 * half
            target = landed.at[slot : slot + half]
        else:
            span = aligned(offset_after(job, b + 1), half)
            source = full.at[span]
            target = full.at[span]
        copy = pltpu.make_async_remote_copy(
            src_ref=source,
            dst_ref=target,
            send_sem=reduce_send.at[job, phase],
            recv_sem=reduce_recv.at[job, phase],
            device_id=(sym, partner),
            device_id_type=MESH,
        )
        copy.start()
        copies[(job, phase)] = copy

    def finish(job, phase):
        base, size = jobs[job]
        copies[(job, phase)].wait()
        if phase < steps:
            half = size >> (phase + 1)
            span = aligned(offset_after(job, phase + 1), half)
            slot = base + size - 2 * half
            target = full if phase == steps - 1 else partial
            target[span, :] = partial[span, :] + landed[slot : slot + half, :]
        if phase + 1 < 2 * steps:
            start(job, phase + 1)

    start(0, 0)
    start(1, 0)

    def project(r, total):
        load(x_hbm, x_buf, x_sem, r).wait()
        return total + contract(split(x_buf[r]), (v_high[r], v_low[r]), ROWS)

    projected = lax.fori_loop(0, blocks, project, jnp.zeros((eig, panels * width), F32))
    for k in range(panels):
        at = coupled_rows + k * eig
        partial[at : at + eig, :] = projected[:, k * width : (k + 1) * width]
    for job in range(2, len(jobs)):
        start(job, 0)

    slots_copy.wait()
    to_smem = pltpu.make_async_copy(slots_vmem, slots_smem, slot_sem.at[2])
    to_smem.start()

    def transfer_matrix():
        for k in reversed(range(panels)):
            here = slice(k * width, (k + 1) * width)
            t_ref[here, here] = f_ref[k]
            if k:
                t_ref[here, : k * width] = jnp.zeros((width, k * width), F32)
            if k < panels - 1:
                later = slice((k + 1) * width, panels * width)
                row = jnp.concatenate(
                    [full[where[(k, j)] : where[(k, j)] + width, :] for j in range(k + 1, panels)],
                    axis=1,
                )
                inner = contract(split(row), split(t_ref[later, later]), PLAIN)
                t_ref[here, later] = -contract(split(f_ref[k]), split(inner), PLAIN)

    for wave in range(2 * steps + len(jobs) - 1):
        for job in range(len(jobs)):
            phase = wave - job
            if 0 <= phase < 2 * steps:
                finish(job, phase)
                if job == 1 and phase == 2 * steps - 1:
                    transfer_matrix()

    gathered = jnp.concatenate(
        [full[coupled_rows + k * eig : coupled_rows + (k + 1) * eig, :] for k in range(panels)],
        axis=1,
    )
    high, low = split(contract(split(t_ref[...]), split(gathered), COLUMNS))
    u_high[...] = high
    u_low[...] = low

    def finished(slot):
        change = contract((v_high[slot], v_low[slot]), (u_high[...], u_low[...]), PLAIN)
        live = lax.broadcasted_iota(jnp.int32, (BLOCK, eig), 0) < channels_ref[0, slot]
        return jnp.where(live, x_buf[slot] - change, 0.0)

    to_smem.wait()
    kets = []
    for t in range(tile_slots):
        ket_out[t] = finished(slots_smem[0, t]).astype(BF16)
        copy = pltpu.make_async_remote_copy(
            src_ref=ket_out.at[t],
            dst_ref=ket_in.at[t],
            send_sem=ket_send.at[t],
            recv_sem=ket_recv.at[t],
            device_id=(before, me),
            device_id_type=MESH,
        )
        copy.start()
        kets.append(copy)
    bras = []
    for t in range(tile_slots):
        occupied = occupied_ref[0, t].astype(F32)
        bras.append((finished(left_ref[0, t]) * occupied).astype(BF16))
    total = jnp.zeros((eig, eig), F32)
    for t in range(tile_slots):
        kets[t].wait()
        product = jnp.dot(tiles_ref[t], ket_in[t], preferred_element_type=F32).astype(BF16)
        total = total + lax.dot_general(
            bras[t], product, (ROWS, ((), ())), preferred_element_type=F32
        )
    share = eig // n
    own[...] = total.reshape(n, share, eig)
    dipole_out[...] = total.reshape(n, share, eig).astype(BF16)
    sends = []
    for d in range(1, n):
        target = lax.rem(me + d, n)
        copy = pltpu.make_async_remote_copy(
            src_ref=dipole_out.at[target],
            dst_ref=dipole_in.at[d - 1],
            send_sem=dipole_send.at[d - 1],
            recv_sem=dipole_recv.at[d - 1],
            device_id=(sym, target),
            device_id_type=MESH,
        )
        copy.start()
        sends.append(copy)
    result = own[me]
    for d in range(1, n):
        sends[d - 1].wait()
        result = result + dipole_in[d - 1].astype(F32)
    out_ref[0] = result


def on_device(
    n,
    syms,
    vectors,
    reflectors,
    factors,
    tiles,
    tile_left,
    tile_right,
    tile_occupied_mask,
    channels,
):
    start = vectors[0]
    panels = reflectors[0]
    rows, eig = start.shape
    count, width, _ = factors.shape[1:]
    tile_slots = tiles.shape[1]
    steps = n.bit_length() - 1
    blocks = rows // BLOCK
    coupled_rows = count * (count - 1) // 2 * width
    reduced = coupled_rows + count * eig
    share = eig // n
    dma = pltpu.SemaphoreType.DMA
    vmem = pl.BlockSpec(memory_space=pltpu.VMEM)
    smem = pl.BlockSpec(memory_space=pltpu.SMEM)
    hbm = pl.BlockSpec(memory_space=pl.ANY)
    return pl.pallas_call(
        functools.partial(kernel, n, syms),
        out_shape=jax.ShapeDtypeStruct((1, share, eig), F32),
        in_specs=[hbm, hbm, vmem, vmem, vmem, smem, smem, smem],
        out_specs=vmem,
        scratch_shapes=[
            pltpu.VMEM((blocks, BLOCK, eig), F32),
            pltpu.VMEM((blocks, BLOCK, count * width), F32),
            pltpu.VMEM((blocks, BLOCK, count * width), BF16),
            pltpu.VMEM((blocks, BLOCK, count * width), BF16),
            pltpu.VMEM((1, tile_slots), jnp.int32),
            pltpu.SMEM((1, tile_slots), jnp.int32),
            pltpu.VMEM((reduced, width), F32),
            pltpu.VMEM((reduced, width), F32),
            pltpu.VMEM((reduced, width), F32),
            pltpu.VMEM((count * width, count * width), F32),
            pltpu.VMEM((count * width, eig), BF16),
            pltpu.VMEM((count * width, eig), BF16),
            pltpu.VMEM((tile_slots, BLOCK, eig), BF16),
            pltpu.VMEM((tile_slots, BLOCK, eig), BF16),
            pltpu.VMEM((n, share, eig), F32),
            pltpu.VMEM((n, share, eig), BF16),
            pltpu.VMEM((n - 1, share, eig), BF16),
            dma((blocks,)),
            dma((blocks,)),
            dma((3,)),
            dma((4, 2 * steps)),
            dma((4, 2 * steps)),
            dma((tile_slots,)),
            dma((tile_slots,)),
            dma((n - 1,)),
            dma((n - 1,)),
        ],
        compiler_params=pltpu.CompilerParams(
            collective_id=0, has_side_effects=True, vmem_limit_bytes=60 * 1024 * 1024
        ),
    )(
        start.reshape(blocks, BLOCK, eig),
        panels.reshape(blocks, BLOCK, count * width),
        factors[0],
        tiles[0],
        tile_right,
        tile_left,
        tile_occupied_mask,
        channels,
    )


def solution(mesh):
    return jax.shard_map(
        functools.partial(on_device, mesh.shape["row"], mesh.shape["sym"]),
        mesh=mesh,
        in_specs=(
            P("sym", "row", None),
            P("sym", "row", None),
            P("sym", None, None, None),
            P("sym", "row", None, None),
            P("sym", "row"),
            P("sym", "row"),
            P("sym", "row"),
            P("sym", "row"),
        ),
        out_specs=P("sym", "row", None),
        check_vma=False,
    )
```

time: 262 us -> 66.5 us (0.25); the launches traced: 259 us -> 66.3 us
  waiting for transfers between devices: 163 us -> 0 us
  Pallas kernels: 0 us -> 64.9 us
  matrix products: 59.3 us -> 0 us
  local copies, waits for them, and re-layouts: 18.3 us -> 1.38 us
  between operations: 13.6 us -> 0.01 us
  other arithmetic: 3.51 us -> 0 us
    psum x2 -> x0, waiting for transfers between devices: 139 us -> none  [the longest x1 71.9 us: on_device(): lax.psum((jnp.concatenate(pieces, axis=0), row_inner(panels, start)), 'row')]
    pallas_call x0 -> x1, Pallas kernels: none -> 64.9 us  [on_device(): pl.pallas_call(functools.partial(kernel, n, syms), out_shape=jax.ShapeDty...]
    dot_general x16 -> x0, matrix products: 59.3 us -> none  [the longest x4 32.3 us: row_inner(): lax.dot_general(first, second, (((0,), (0,)), ((), ())), precision=PRECISE)]
    ppermute x1 -> x0, waiting for transfers between devices: 23.7 us -> none  [passed_along(): return lax.ppermute(block, axis, route)]
    reshape x2 -> x0, local copies, waits for them, and re-layouts: 5.64 us -> none  [the longest x1 5.63 us: on_device(): result.reshape(-1, BLOCK, eigen_count) * keeper[:, :, None]]
    unnamed x16 -> x1, local copies, waits for them, and re-layouts: 5.78 us -> 1.38 us
    gather x2 -> x0, local copies, waits for them, and re-layouts: 3.54 us -> none  [the longest x1 2.17 us: on_device(): right_rows = jnp.take(remote, slots, axis=0)]
    convert_element_type x3 -> x0, other arithmetic: 2.7 us -> none  [the longest x1 2.63 us: on_device(): (result.reshape(-1, BLOCK, eigen_count) * keeper[:, :, None]).astype(jnp....]
  transfers between devices with their start and end apart: 3 -> 0, of which waited for: 3 -> 0; matrix products, arithmetic and copies ran while one was open for 3% -> 0% of each run, Pallas kernels for 0% -> 0%
where the time goes in v1:
time: 66.5 us; the launch traced here: 66.3 us
  Pallas kernels  64.9 us (98%)
  local copies, waits for them, and re-layouts  1.38 us (2%)
    pallas_call x1, Pallas kernels, on_device(): pl.pallas_call(functools.partial(kernel, n, syms), out_shape=jax.ShapeDty...  64.9 us
    unnamed x1, local copies, waits for them, and re-layouts  1.38 us

profile of v1, /device:TPU:1, one launch (start us, length us, event | category | flops | bytes accessed | tf_op | source)
XLA Modules:
  0.0 66.3 jit_solution(9899237640325370323)
XLA Ops:
  0.0 64.9 %shard_map.82 = f32[1,32,256]{2,1,0:T(8,128)} custom-call(f32[8,512,256]{2,1,0:T(8,128)} %bitcast.5, f32[8,512,512]{2,1,0:T(8,128)} %bitcast.4, f32[4,128,128]{2,1,0:T(8,128)} %bitcast.7, bf16[2,512,512]{2,1,0:T(8,128)(2,1)} %bitcast.6, s32[1,2]{1,0:T(1,128)} %right_ref.1, s32[1,2]{1,0:T(1,128)} %left_ref.1, s32[1,2]{1,0:T(1,128)} %occupied_ref.1, ...), custom_call_target="tpu_custom_call" | custom-call | tf_op jit(solution)/shard_map/pallas_call | solution.py:333
  64.9 1.4 %copy.10 = f32[1,32,256]{2,1,0:T(8,128)} copy(f32[1,32,256]{2,1,0:T(8,128)} %shard_map.82) | data formatting | bytes 65536

commit v2 on v1

v2 whole, which is shorter than its diff:
```python
import functools

import jax
import jax.numpy as jnp
from jax import lax
from jax.experimental import pallas as pl
from jax.experimental.pallas import tpu as pltpu
from jax.sharding import PartitionSpec as P

BLOCK = 512
LANES = 128
JOB_ROWS = 256
SKEW = 3
F32 = jnp.float32
BF16 = jnp.bfloat16
MESH = pl.DeviceIdType.MESH


def split(value):
    high = value.astype(BF16)
    return high, (value - high.astype(F32)).astype(BF16)


def contract(first, second, dims):
    high, low = first
    other_high, other_low = second

    def dot(a, b):
        return lax.dot_general(a, b, (dims, ((), ())), preferred_element_type=F32)

    return dot(high, other_high) + (dot(high, other_low) + dot(low, other_high))


ROWS = ((0,), (0,))
PLAIN = ((1,), (0,))
COLUMNS = ((1,), (1,))


def coupled_ranges(first, count):
    if count < 2:
        return []
    half = count // 2
    here = [(first, half, first + half, count - half)]
    return here + coupled_ranges(first, half) + coupled_ranges(first + half, count - half)


def radices(n):
    bits = n.bit_length() - 1
    return [2] * (bits % 2) + [4] * (bits // 2)


def kernel(
    n,
    syms,
    x_hbm,
    v_hbm,
    f_ref,
    tiles_ref,
    right_ref,
    left_ref,
    occupied_ref,
    channels_ref,
    out_ref,
    x_buf,
    v_buf,
    v_high,
    v_low,
    slots_vmem,
    slots_smem,
    partial,
    landed,
    full,
    t_ref,
    u_high,
    u_low,
    ket_out,
    ket_in,
    bras,
    own,
    dipole_out,
    dipole_in,
    x_sem,
    v_sem,
    slot_sem,
    reduce_send,
    reduce_recv,
    ket_send,
    ket_recv,
    dipole_send,
    dipole_recv,
):
    panels, width, _ = f_ref.shape
    blocks, _, eig = x_buf.shape
    tile_slots = tiles_ref.shape[0]
    halves = eig // LANES
    sym = lax.axis_index("sym")
    me = lax.axis_index("row")
    after = lax.rem(sym + 1, syms)
    before = lax.rem(sym + syms - 1, syms)

    def load(source, target, sems, r):
        return pltpu.make_async_copy(source.at[r], target.at[r], sems.at[r])

    for r in range(blocks):
        load(v_hbm, v_buf, v_sem, r).start()
    for r in range(blocks):
        load(x_hbm, x_buf, x_sem, r).start()

    barrier = pltpu.get_barrier_semaphore()
    for d in range(1, n):
        pl.semaphore_signal(
            barrier, inc=1, device_id=(sym, lax.rem(me + d, n)), device_id_type=MESH
        )
    for other in (after, before):
        pl.semaphore_signal(barrier, inc=1, device_id=(other, me), device_id_type=MESH)
    pl.semaphore_wait(barrier, n + 1)

    slots_copy = pltpu.make_async_remote_copy(
        src_ref=right_ref,
        dst_ref=slots_vmem,
        send_sem=slot_sem.at[0],
        recv_sem=slot_sem.at[1],
        device_id=(after, me),
        device_id_type=MESH,
    )
    slots_copy.start()

    ranges = coupled_ranges(0, panels)

    def couple(r, sums):
        load(v_hbm, v_buf, v_sem, r).wait()
        high, low = split(v_buf[r])
        v_high[r] = high
        v_low[r] = low
        out = []
        for total, (a, ca, b, cb) in zip(sums, ranges):
            pa = slice(a * width, (a + ca) * width)
            pb = slice(b * width, (b + cb) * width)
            out.append(
                total + contract((high[:, pa], low[:, pa]), (high[:, pb], low[:, pb]), ROWS)
            )
        return tuple(out)

    sums = lax.fori_loop(
        0, blocks, couple, tuple(jnp.zeros((ca * width, cb * width), F32) for _, ca, _, cb in ranges)
    )
    where = {}
    place = 0
    for total, (a, ca, b, cb) in zip(sums, ranges):
        for i in range(ca):
            for j in range(cb):
                where[(a + i, b + j)] = place
                partial[place : place + width, :] = total[
                    i * width : (i + 1) * width, j * width : (j + 1) * width
                ]
                place = place + width
    coupled_rows = place
    total_rows = coupled_rows + panels * eig
    job_rows = max(JOB_ROWS, 8 * n)
    job_count = total_rows // job_rows
    coupled_jobs = coupled_rows // job_rows
    jobs_of_half = (job_count - coupled_jobs) // halves

    copies = {}
    factors = radices(n)
    levels = len(factors)
    strides = [1]
    sizes = [job_rows]
    for radix in factors:
        strides.append(strides[-1] * radix)
        sizes.append(sizes[-1] // radix)
    slots = [0]
    for radix, size in zip(factors, sizes[1:]):
        slots.append(slots[-1] + (radix - 1) * size)

    def digit(level):
        return lax.rem(me // strides[level], factors[level])

    def span_after(job, level, last=None):
        offset = job * job_rows
        for below in range(level):
            place = digit(below) if last is None or below < level - 1 else last
            offset = offset + place * sizes[below + 1]
        return pl.ds(pl.multiple_of(offset, 8), sizes[level])

    def start(job, phase):
        level = phase if phase < levels else 2 * levels - 1 - phase
        radix = factors[level]
        piece = sizes[level + 1]
        copies[(job, phase)] = []
        for k in range(1, radix):
            other = lax.rem(digit(level) + k, radix)
            if phase < levels:
                source = partial.at[span_after(job, level + 1, other)]
                slot = job * job_rows + slots[level] + (k - 1) * piece
                target = landed.at[slot : slot + piece]
            else:
                source = full.at[span_after(job, level + 1)]
                target = source
            copy = pltpu.make_async_remote_copy(
                src_ref=source,
                dst_ref=target,
                send_sem=reduce_send.at[job, phase, k - 1],
                recv_sem=reduce_recv.at[job, phase, k - 1],
                device_id=(sym, me + (other - digit(level)) * strides[level]),
                device_id_type=MESH,
            )
            copy.start()
            copies[(job, phase)].append(copy)

    def finish(job, phase):
        for copy in copies[(job, phase)]:
            copy.wait()
        if phase < levels:
            piece = sizes[phase + 1]
            span = span_after(job, phase + 1)
            value = partial[span, :]
            for k in range(1, factors[phase]):
                slot = job * job_rows + slots[phase] + (k - 1) * piece
                value = value + landed[slot : slot + piece, :]
            target = full if phase == levels - 1 else partial
            target[span, :] = value
        if phase + 1 < 2 * levels:
            start(job, phase + 1)

    for job in range(coupled_jobs):
        start(job, 0)

    def project(r, total):
        load(x_hbm, x_buf, x_sem, r).wait()
        return total + contract(split(x_buf[r]), (v_high[r], v_low[r]), ROWS)

    projected = lax.fori_loop(0, blocks, project, jnp.zeros((eig, panels * width), F32))
    for h in range(halves):
        for k in range(panels):
            at = coupled_rows + (h * panels + k) * LANES
            partial[at : at + LANES, :] = projected[
                h * LANES : (h + 1) * LANES, k * width : (k + 1) * width
            ]
    for job in range(coupled_jobs, job_count):
        start(job, 0)

    slots_copy.wait()
    to_smem = pltpu.make_async_copy(slots_vmem, slots_smem, slot_sem.at[2])
    to_smem.start()

    def transfer_matrix():
        for k in reversed(range(panels)):
            here = slice(k * width, (k + 1) * width)
            t_ref[here, here] = f_ref[k]
            if k:
                t_ref[here, : k * width] = jnp.zeros((width, k * width), F32)
            if k < panels - 1:
                later = slice((k + 1) * width, panels * width)
                row = jnp.concatenate(
                    [full[where[(k, j)] : where[(k, j)] + width, :] for j in range(k + 1, panels)],
                    axis=1,
                )
                inner = contract(split(row), split(t_ref[later, later]), PLAIN)
                t_ref[here, later] = -contract(split(f_ref[k]), split(inner), PLAIN)

    def update(h):
        begin = coupled_rows + h * panels * LANES
        gathered = jnp.concatenate(
            [full[begin + k * LANES : begin + (k + 1) * LANES, :] for k in range(panels)], axis=1
        )
        high, low = split(contract(split(t_ref[...]), split(gathered), COLUMNS))
        u_high[h] = high
        u_low[h] = low

    def finished(slot, h):
        change = contract((v_high[slot], v_low[slot]), (u_high[h], u_low[h]), PLAIN)
        live = lax.broadcasted_iota(jnp.int32, (BLOCK, LANES), 0) < channels_ref[0, slot]
        value = x_buf[slot, :, h * LANES : (h + 1) * LANES] - change
        return jnp.where(live, value, 0.0)

    kets = {}

    def right_blocks(h):
        for t in range(tile_slots):
            ket_out[h, t] = finished(slots_smem[0, t], h).astype(BF16)
            copy = pltpu.make_async_remote_copy(
                src_ref=ket_out.at[h, t],
                dst_ref=ket_in.at[h, t],
                send_sem=ket_send.at[h, t],
                recv_sem=ket_recv.at[h, t],
                device_id=(before, me),
                device_id_type=MESH,
            )
            copy.start()
            kets[(h, t)] = copy

    def left_blocks(h):
        for t in range(tile_slots):
            occupied = occupied_ref[0, t].astype(F32)
            bras[t, :, h * LANES : (h + 1) * LANES] = (
                finished(left_ref[0, t], h) * occupied
            ).astype(BF16)

    to_smem.wait()
    events = [(job + SKEW * phase, job, phase) for job in range(job_count) for phase in range(2 * levels)]
    for _, job, phase in sorted(events):
        finish(job, phase)
        if phase == 2 * levels - 1:
            if job == coupled_jobs - 1:
                transfer_matrix()
            done = job + 1 - coupled_jobs
            if done > 0 and done % jobs_of_half == 0:
                h = done // jobs_of_half - 1
                update(h)
                right_blocks(h)
                if h < halves - 1:
                    left_blocks(h)
    left_blocks(halves - 1)

    share = eig // n
    sends = []
    for h in range(halves):
        total = jnp.zeros((eig, LANES), F32)
        for t in range(tile_slots):
            kets[(h, t)].wait()
            product = jnp.dot(tiles_ref[t], ket_in[h, t], preferred_element_type=F32).astype(BF16)
            total = total + lax.dot_general(
                bras[t], product, (ROWS, ((), ())), preferred_element_type=F32
            )
        own[h] = total.reshape(n, share, LANES)
        dipole_out[h] = total.reshape(n, share, LANES).astype(BF16)
        for d in range(1, n):
            target = lax.rem(me + d, n)
            copy = pltpu.make_async_remote_copy(
                src_ref=dipole_out.at[h, target],
                dst_ref=dipole_in.at[h, d - 1],
                send_sem=dipole_send.at[h, d - 1],
                recv_sem=dipole_recv.at[h, d - 1],
                device_id=(sym, target),
                device_id_type=MESH,
            )
            copy.start()
            sends.append((h, d, copy))
    results = [own[h, me] for h in range(halves)]
    for h, d, copy in sends:
        copy.wait()
        results[h] = results[h] + dipole_in[h, d - 1].astype(F32)
    for h in range(halves):
        out_ref[0, :, h * LANES : (h + 1) * LANES] = results[h]


def on_device(
    n,
    syms,
    vectors,
    reflectors,
    factors,
    tiles,
    tile_left,
    tile_right,
    tile_occupied_mask,
    channels,
):
    start = vectors[0]
    panels = reflectors[0]
    rows, eig = start.shape
    count, width, _ = factors.shape[1:]
    tile_slots = tiles.shape[1]
    halves = eig // LANES
    phases = 2 * len(radices(n))
    peers = max(radices(n)) - 1
    blocks = rows // BLOCK
    coupled_rows = count * (count - 1) // 2 * width
    reduced = coupled_rows + count * eig
    jobs = reduced // max(JOB_ROWS, 8 * n)
    share = eig // n
    dma = pltpu.SemaphoreType.DMA
    vmem = pl.BlockSpec(memory_space=pltpu.VMEM)
    smem = pl.BlockSpec(memory_space=pltpu.SMEM)
    hbm = pl.BlockSpec(memory_space=pl.ANY)
    return pl.pallas_call(
        functools.partial(kernel, n, syms),
        out_shape=jax.ShapeDtypeStruct((1, share, eig), F32),
        in_specs=[hbm, hbm, vmem, vmem, vmem, smem, smem, smem],
        out_specs=vmem,
        scratch_shapes=[
            pltpu.VMEM((blocks, BLOCK, eig), F32),
            pltpu.VMEM((blocks, BLOCK, count * width), F32),
            pltpu.VMEM((blocks, BLOCK, count * width), BF16),
            pltpu.VMEM((blocks, BLOCK, count * width), BF16),
            pltpu.VMEM((1, tile_slots), jnp.int32),
            pltpu.SMEM((1, tile_slots), jnp.int32),
            pltpu.VMEM((reduced, width), F32),
            pltpu.VMEM((reduced, width), F32),
            pltpu.VMEM((reduced, width), F32),
            pltpu.VMEM((count * width, count * width), F32),
            pltpu.VMEM((halves, count * width, LANES), BF16),
            pltpu.VMEM((halves, count * width, LANES), BF16),
            pltpu.VMEM((halves, tile_slots, BLOCK, LANES), BF16),
            pltpu.VMEM((halves, tile_slots, BLOCK, LANES), BF16),
            pltpu.VMEM((tile_slots, BLOCK, eig), BF16),
            pltpu.VMEM((halves, n, share, LANES), F32),
            pltpu.VMEM((halves, n, share, LANES), BF16),
            pltpu.VMEM((halves, n - 1, share, LANES), BF16),
            dma((blocks,)),
            dma((blocks,)),
            dma((3,)),
            dma((jobs, phases, peers)),
            dma((jobs, phases, peers)),
            dma((halves, tile_slots)),
            dma((halves, tile_slots)),
            dma((halves, n - 1)),
            dma((halves, n - 1)),
        ],
        compiler_params=pltpu.CompilerParams(
            collective_id=0, has_side_effects=True, vmem_limit_bytes=60 * 1024 * 1024
        ),
    )(
        start.reshape(blocks, BLOCK, eig),
        panels.reshape(blocks, BLOCK, count * width),
        factors[0],
        tiles[0],
        tile_right,
        tile_left,
        tile_occupied_mask,
        channels,
    )


def solution(mesh):
    return jax.shard_map(
        functools.partial(on_device, mesh.shape["row"], mesh.shape["sym"]),
        mesh=mesh,
        in_specs=(
            P("sym", "row", None),
            P("sym", "row", None),
            P("sym", None, None, None),
            P("sym", "row", None, None),
            P("sym", "row"),
            P("sym", "row"),
            P("sym", "row"),
            P("sym", "row"),
        ),
        out_specs=P("sym", "row", None),
        check_vma=False,
    )
```

time: 66.5 us -> 61.3 us (0.922)
  Pallas kernels: 64.9 us -> 59.8 us
    pallas_call x1, Pallas kernels: 64.9 us -> 59.8 us  [on_device(): pl.pallas_call(functools.partial(kernel, n, syms), out_shape=jax.ShapeDty...]
where the time goes in v2:
time: 61.3 us; the launch traced here: 61.1 us
  Pallas kernels  59.8 us (98%)
  local copies, waits for them, and re-layouts  1.38 us (2%)
    pallas_call x1, Pallas kernels, on_device(): pl.pallas_call(functools.partial(kernel, n, syms), out_shape=jax.ShapeDty...  59.8 us
    unnamed x1, local copies, waits for them, and re-layouts  1.38 us

profile of v2, /device:TPU:1, one launch (start us, length us, event | category | flops | bytes accessed | tf_op | source)
XLA Modules:
  0.0 61.1 jit_solution(18371118944546386622)
XLA Ops:
  0.0 59.8 %shard_map.82 = f32[1,32,256]{2,1,0:T(8,128)} custom-call(f32[8,512,256]{2,1,0:T(8,128)} %bitcast.5, f32[8,512,512]{2,1,0:T(8,128)} %bitcast.4, f32[4,128,128]{2,1,0:T(8,128)} %bitcast.7, bf16[2,512,512]{2,1,0:T(8,128)(2,1)} %bitcast.6, s32[1,2]{1,0:T(1,128)} %right_ref.1, s32[1,2]{1,0:T(1,128)} %left_ref.1, s32[1,2]{1,0:T(1,128)} %occupied_ref.1, ...), custom_call_target="tpu_custom_call" | custom-call | tf_op jit(solution)/shard_map/pallas_call | solution.py:377
  59.8 1.4 %copy.10 = f32[1,32,256]{2,1,0:T(8,128)} copy(f32[1,32,256]{2,1,0:T(8,128)} %shard_map.82) | data formatting | bytes 65536

commit v3 on v2

--- a/solution.py
+++ b/solution.py
@@ -11,6 +11,8 @@
 LANES = 128
 JOB_ROWS = 256
 SKEW = 3
+SWAPPED = (1, 3, 5)
+EARLY = ((), ((0, 0),), ((1, 0),))
 F32 = jnp.float32
 BF16 = jnp.bfloat16
 MESH = pl.DeviceIdType.MESH
@@ -44,9 +46,11 @@
     return here + coupled_ranges(first, half) + coupled_ranges(first + half, count - half)
 
 
-def radices(n):
-    bits = n.bit_length() - 1
-    return [2] * (bits % 2) + [4] * (bits // 2)
+def exchanges(n, job):
+    strides = [1 << bit for bit in range(n.bit_length() - 1)]
+    if job in SWAPPED and len(strides) > 1:
+        strides[:2] = strides[1::-1]
+    return strides
 
 
 def kernel(
@@ -54,8 +58,8 @@
     syms,
     x_hbm,
     v_hbm,
-    f_ref,
-    tiles_ref,
+    f_hbm,
+    tiles_hbm,
     right_ref,
     left_ref,
     occupied_ref,
@@ -79,9 +83,12 @@
     own,
     dipole_out,
     dipole_in,
+    f_ref,
+    tiles_ref,
     x_sem,
     v_sem,
     slot_sem,
+    operand_sem,
     reduce_send,
     reduce_recv,
     ket_send,
@@ -105,6 +112,11 @@
         load(v_hbm, v_buf, v_sem, r).start()
     for r in range(blocks):
         load(x_hbm, x_buf, x_sem, r).start()
+
+    f_copy = pltpu.make_async_copy(f_hbm, f_ref, operand_sem.at[0])
+    f_copy.start()
+    tiles_copy = pltpu.make_async_copy(tiles_hbm, tiles_ref, operand_sem.at[1])
+    tiles_copy.start()
 
     barrier = pltpu.get_barrier_semaphore()
     for d in range(1, n):
@@ -162,64 +174,51 @@
     jobs_of_half = (job_count - coupled_jobs) // halves
 
     copies = {}
-    factors = radices(n)
-    levels = len(factors)
-    strides = [1]
-    sizes = [job_rows]
-    for radix in factors:
-        strides.append(strides[-1] * radix)
-        sizes.append(sizes[-1] // radix)
-    slots = [0]
-    for radix, size in zip(factors, sizes[1:]):
-        slots.append(slots[-1] + (radix - 1) * size)
-
-    def digit(level):
-        return lax.rem(me // strides[level], factors[level])
-
-    def span_after(job, level, last=None):
+    levels = n.bit_length() - 1
+
+    def digit(job, level):
+        return lax.rem(me // exchanges(n, job)[level], 2)
+
+    def span_after(job, level, flip=False):
         offset = job * job_rows
         for below in range(level):
-            place = digit(below) if last is None or below < level - 1 else last
-            offset = offset + place * sizes[below + 1]
-        return pl.ds(pl.multiple_of(offset, 8), sizes[level])
+            place = digit(job, below)
+            if flip and below == level - 1:
+                place = 1 - place
+            offset = offset + place * (job_rows >> (below + 1))
+        return pl.ds(pl.multiple_of(offset, 8), job_rows >> level)
+
+    def landing(job, level):
+        piece = job_rows >> (level + 1)
+        slot = (job + 1) * job_rows - 2 * piece
+        return slice(slot, slot + piece)
 
     def start(job, phase):
         level = phase if phase < levels else 2 * levels - 1 - phase
-        radix = factors[level]
-        piece = sizes[level + 1]
-        copies[(job, phase)] = []
-        for k in range(1, radix):
-            other = lax.rem(digit(level) + k, radix)
-            if phase < levels:
-                source = partial.at[span_after(job, level + 1, other)]
-                slot = job * job_rows + slots[level] + (k - 1) * piece
-                target = landed.at[slot : slot + piece]
-            else:
-                source = full.at[span_after(job, level + 1)]
-                target = source
-            copy = pltpu.make_async_remote_copy(
-                src_ref=source,
-                dst_ref=target,
-                send_sem=reduce_send.at[job, phase, k - 1],
-                recv_sem=reduce_recv.at[job, phase, k - 1],
-                device_id=(sym, me + (other - digit(level)) * strides[level]),
-                device_id_type=MESH,
-            )
-            copy.start()
-            copies[(job, phase)].append(copy)
+        if phase < levels:
+            source = partial.at[span_after(job, level + 1, True)]
+            target = landed.at[landing(job, level)]
+        else:
+            source = full.at[span_after(job, level + 1)]
+            target = source
+        partner = me + (1 - 2 * digit(job, level)) * exchanges(n, job)[level]
+        copy = pltpu.make_async_remote_copy(
+            src_ref=source,
+            dst_ref=target,
+            send_sem=reduce_send.at[job, phase],
+            recv_sem=reduce_recv.at[job, phase],
+            device_id=(sym, partner),
+            device_id_type=MESH,
+        )
+        copy.start()
+        copies[(job, phase)] = copy
 
     def finish(job, phase):
-        for copy in copies[(job, phase)]:
-            copy.wait()
+        copies[(job, phase)].wait()
         if phase < levels:
-            piece = sizes[phase + 1]
             span = span_after(job, phase + 1)
-            value = partial[span, :]
-            for k in range(1, factors[phase]):
-                slot = job * job_rows + slots[phase] + (k - 1) * piece
-                value = value + landed[slot : slot + piece, :]
             target = full if phase == levels - 1 else partial
-            target[span, :] = value
+            target[span, :] = partial[span, :] + landed[landing(job, phase), :]
         if phase + 1 < 2 * levels:
             start(job, phase + 1)
 
@@ -230,7 +229,15 @@
         load(x_hbm, x_buf, x_sem, r).wait()
         return total + contract(split(x_buf[r]), (v_high[r], v_low[r]), ROWS)
 
-    projected = lax.fori_loop(0, blocks, project, jnp.zeros((eig, panels * width), F32))
+    projected = jnp.zeros((eig, panels * width), F32)
+    parts = len(EARLY) + 1
+    for part in range(parts):
+        projected = lax.fori_loop(
+            part * blocks // parts, (part + 1) * blocks // parts, project, projected
+        )
+        if part < parts - 1:
+            for job, phase in EARLY[part]:
+                finish(job, phase)
     for h in range(halves):
         for k in range(panels):
             at = coupled_rows + (h * panels + k) * LANES
@@ -245,6 +252,7 @@
     to_smem.start()
 
     def transfer_matrix():
+        f_copy.wait()
         for k in reversed(range(panels)):
             here = slice(k * width, (k + 1) * width)
             t_ref[here, here] = f_ref[k]
@@ -299,8 +307,10 @@
 
     to_smem.wait()
     events = [(job + SKEW * phase, job, phase) for job in range(job_count) for phase in range(2 * levels)]
+    early = [event for part in EARLY for event in part]
     for _, job, phase in sorted(events):
-        finish(job, phase)
+        if (job, phase) not in early:
+            finish(job, phase)
         if phase == 2 * levels - 1:
             if job == coupled_jobs - 1:
                 transfer_matrix()
@@ -314,6 +324,7 @@
     left_blocks(halves - 1)
 
     share = eig // n
+    tiles_copy.wait()
     sends = []
     for h in range(halves):
         total = jnp.zeros((eig, LANES), F32)
@@ -363,8 +374,7 @@
     count, width, _ = factors.shape[1:]
     tile_slots = tiles.shape[1]
     halves = eig // LANES
-    phases = 2 * len(radices(n))
-    peers = max(radices(n)) - 1
+    phases = 2 * (n.bit_length() - 1)
     blocks = rows // BLOCK
     coupled_rows = count * (count - 1) // 2 * width
     reduced = coupled_rows + count * eig
@@ -377,7 +387,7 @@
     return pl.pallas_call(
         functools.partial(kernel, n, syms),
         out_shape=jax.ShapeDtypeStruct((1, share, eig), F32),
-        in_specs=[hbm, hbm, vmem, vmem, vmem, smem, smem, smem],
+        in_specs=[hbm, hbm, hbm, hbm, vmem, smem, smem, smem],
         out_specs=vmem,
         scratch_shapes=[
             pltpu.VMEM((blocks, BLOCK, eig), F32),
@@ -398,11 +408,14 @@
             pltpu.VMEM((halves, n, share, LANES), F32),
             pltpu.VMEM((halves, n, share, LANES), BF16),
             pltpu.VMEM((halves, n - 1, share, LANES), BF16),
+            pltpu.VMEM((count, width, width), F32),
+            pltpu.VMEM((tile_slots, BLOCK, BLOCK), BF16),
             dma((blocks,)),
             dma((blocks,)),
             dma((3,)),
-            dma((jobs, phases, peers)),
-            dma((jobs, phases, peers)),
+            dma((2,)),
+            dma((jobs, phases)),
+            dma((jobs, phases)),
             dma((halves, tile_slots)),
             dma((halves, tile_slots)),
             dma((halves, n - 1)),

time: 61.3 us -> 58.3 us (0.951)
  Pallas kernels: 59.8 us -> 56.8 us
    pallas_call x1, Pallas kernels: 59.8 us -> 56.8 us  [on_device(): pl.pallas_call(functools.partial(kernel, n, syms), out_shape=jax.ShapeDty...]
where the time goes in v3:
time: 58.3 us; the launch traced here: 58.1 us
  Pallas kernels  56.8 us (97%)
  local copies, waits for them, and re-layouts  1.38 us (2%)
    pallas_call x1, Pallas kernels, on_device(): pl.pallas_call(functools.partial(kernel, n, syms), out_shape=jax.ShapeDty...  56.8 us
    unnamed x1, local copies, waits for them, and re-layouts  1.38 us

profile of v3, /device:TPU:1, one launch (start us, length us, event | category | flops | bytes accessed | tf_op | source)
XLA Modules:
  0.0 58.1 jit_solution(9246811323659743663)
XLA Ops:
  0.0 56.8 %shard_map.82 = f32[1,32,256]{2,1,0:T(8,128)} custom-call(f32[8,512,256]{2,1,0:T(8,128)} %bitcast.5, f32[8,512,512]{2,1,0:T(8,128)} %bitcast.4, f32[4,128,128]{2,1,0:T(8,128)} %bitcast.7, bf16[2,512,512]{2,1,0:T(8,128)(2,1)} %bitcast.6, s32[1,2]{1,0:T(1,128)} %right_ref.1, s32[1,2]{1,0:T(1,128)} %left_ref.1, s32[1,2]{1,0:T(1,128)} %occupied_ref.1, ...), custom_call_target="tpu_custom_call" | custom-call | tf_op jit(solution)/shard_map/pallas_call | solution.py:387
  56.8 1.4 %copy.10 = f32[1,32,256]{2,1,0:T(8,128)} copy(f32[1,32,256]{2,1,0:T(8,128)} %shard_map.82) | data formatting | bytes 65536
